TPU v7x, 32 devices: a whole 2x2x4 slice. The times are simulated.
32 devices in a mesh: seg: 8 (over z, core), seq: 4 (over y, x).
Axes of the slice: x: 2, y: 2, z: 4, core: 2. Of those that a mesh axis runs over, the one named last changes fastest.
Arguments:
- layer_input: bfloat16 [8, 2048, 1024], P('seg', 'seq'), may hold values from -6 to 6
- output_grad: bfloat16 [8, 2048, 1024], P('seg', 'seq'), may hold values from -6 to 6
- norm1_gain: float32 [1024], replicated, may hold values from 0.5 to 1.5
- norm2_gain: float32 [1024], replicated, may hold values from 0.5 to 1.5
- w_qkv: bfloat16 [1024, 3072], replicated, may hold values from -0.25 to 0.25
- w_out: bfloat16 [1024, 1024], replicated, may hold values from -0.75 to 0.75
- w_gate: bfloat16 [1024, 2816], replicated, may hold values from -0.1875 to 0.1875
- w_up: bfloat16 [1024, 2816], replicated, may hold values from -0.1875 to 0.1875
- w_down: bfloat16 [2816, 1024], replicated, may hold values from -0.109375 to 0.109375
- mem_keys: bfloat16 [8, 1024, 1024], P('seg', 'seq'), may hold values from -8 to 8
- mem_values: bfloat16 [8, 1024, 1024], P('seg', 'seq'), may hold values from -8 to 8
- memory_flags: int32 [8], replicated, may hold values from 0 to 1, as said below
- sources: int32 [8, 3], replicated, may hold values from 0 to 7, as said below
Outputs:
- output: bfloat16 [8, 2048, 1024], P('seg', 'seq')
- input_grad: float32 [8, 2048, 1024], P('seg', 'seq')
- grad_norm1: float32 [1024], P('seq')
- grad_norm2: float32 [1024], P('seq')
- grad_qkv: float32 [1024, 3072], P('seq')
- grad_out: float32 [1024, 1024], P('seq')
- grad_gate: float32 [1024, 2816], P('seq')
- grad_up: float32 [1024, 2816], P('seq')
- grad_down: float32 [2816, 1024], P('seq')
Inputs may be any that keep to these rules, and one draw needn't show every extreme that they name: `memory_flags`: exactly half of the segments have flag 1. `sources`: row s lists 3 different segments, none of them s. The first column is a permutation of the segments, and the first source of a segment has the other flag than the segment.
All inputs are finite; a program needn't handle non-finite values.
Results may differ from a plain program's by a relative error of at most 0.023.
Values may be sent and summed in bfloat16 or wider, within the bound.
A program may use at most 256 MiB of HBM per device.

v0:
```python
import jax
import jax.numpy as jnp
from jax import lax
from jax.sharding import PartitionSpec as P

D = 1024
HEADS = 8
HEAD_DIM = 128


masked_score = -1e30
epsilon = 1e-06
rotary_base = 10000.0


def product(former, latter):
    return jnp.dot(former, latter, preferred_element_type=jnp.float32)


def product_nt(former, latter):
    return lax.dot_general(
        former, latter, (((1,), (1,)), ((), ())), preferred_element_type=jnp.float32
    )


def product_tn(former, latter):
    return lax.dot_general(
        former, latter, (((0,), (0,)), ((), ())), preferred_element_type=jnp.float32
    )


def norm_forward(values, norm_gain):
    inverse = lax.rsqrt(jnp.mean(values * values, axis=-1, keepdims=True) + epsilon)
    return (values * inverse * norm_gain, inverse)


def norm_backward(values, inverse, norm_gain, upstream):
    weighted = upstream * norm_gain
    inner_mean = jnp.mean(weighted * values, axis=-1, keepdims=True)
    grad_values = inverse * weighted - inverse * inverse * inverse * values * inner_mean
    grad_gain = jnp.sum(upstream * values * inverse, axis=0)
    return (grad_values, grad_gain)


def turn_tables(positions):
    half_dim = HEAD_DIM // 2
    exponent = -2.0 * jnp.arange(half_dim, dtype=jnp.float32) / HEAD_DIM
    angles = positions[:, None] * jnp.power(rotary_base, exponent)[None, :]
    angles = jnp.concatenate([angles, angles], axis=1)
    return (jnp.cos(angles)[:, None, :], jnp.sin(angles)[:, None, :])


def rotate(matrix, cosine_table, sine_table, direction):
    row_count = matrix.shape[0]
    half_dim = HEAD_DIM // 2
    shaped = matrix.reshape(row_count, HEADS, HEAD_DIM)
    turned = jnp.concatenate([-shaped[..., half_dim:], shaped[..., :half_dim]], axis=-1)
    return (shaped * cosine_table + direction * turned * sine_table).reshape(
        row_count, HEADS * HEAD_DIM
    )


def on_device(
    layer_input,
    output_grad,
    norm1_gain,
    norm2_gain,
    w_qkv,
    w_out,
    w_gate,
    w_up,
    w_down,
    mem_keys,
    mem_values,
    memory_flags,
    sources,
):
    seg_index = lax.axis_index("seg")
    seq_index = lax.axis_index("seq")
    tokens = layer_input.shape[1]
    score_scale = HEAD_DIM ** (-0.5)
    flag_on = lax.dynamic_index_in_dim(memory_flags, seg_index, 0, keepdims=False) > 0
    listed = lax.dynamic_index_in_dim(sources, seg_index, 0, keepdims=False)
    picked = jnp.concatenate([jnp.reshape(seg_index, (1,)), listed])
    every_keys, every_values = (
        lax.all_gather(mem_keys, "seg", axis=0, tiled=True),
        lax.all_gather(mem_values, "seg", axis=0, tiled=True),
    )
    chosen_keys = jnp.take(every_keys, picked, axis=0)
    chosen_values = jnp.take(every_values, picked, axis=0)
    memory_keys, memory_values = (
        lax.all_gather(chosen_keys, "seq", axis=1, tiled=True),
        lax.all_gather(chosen_values, "seq", axis=1, tiled=True),
    )
    memory_key_blocks = memory_keys.reshape(-1, tokens, HEADS, HEAD_DIM)
    memory_value_blocks = memory_values.reshape(-1, tokens, HEADS, HEAD_DIM)
    memory_blocks = memory_key_blocks.shape[0]
    inputs = layer_input[0].astype(jnp.float32)
    first_norm, first_inverse = norm_forward(inputs, norm1_gain)
    first_low = first_norm.astype(jnp.bfloat16)
    projected = product(first_low, w_qkv)
    positions = seq_index * tokens + lax.iota(jnp.int32, tokens)
    cosine_table, sine_table = turn_tables(positions.astype(jnp.float32))
    queries = rotate(projected[:, :D], cosine_table, sine_table, 1.0).astype(jnp.bfloat16)
    own_keys = rotate(projected[:, D : 2 * D], cosine_table, sine_table, 1.0).astype(jnp.bfloat16)
    own_values = projected[:, 2 * D :].astype(jnp.bfloat16)
    all_keys, all_values = (
        lax.all_gather(own_keys, "seq", axis=0, tiled=True),
        lax.all_gather(own_values, "seq", axis=0, tiled=True),
    )
    key_blocks = all_keys.reshape(-1, tokens, HEADS, HEAD_DIM)
    value_blocks = all_values.reshape(-1, tokens, HEADS, HEAD_DIM)
    query_heads = queries.reshape(tokens, HEADS, HEAD_DIM)
    memory_open = jnp.broadcast_to(flag_on, (tokens, tokens))
    own_count = seq_index + 1
    key_offsets = lax.iota(jnp.int32, tokens)

    def own_open(block):
        return (block * tokens + key_offsets)[None, :] <= positions[:, None]

    def block_scores(key_block, open_mask):
        raw = (
            jnp.einsum("qhd,khd->hqk", query_heads, key_block, preferred_element_type=jnp.float32)
            * score_scale
        )
        return jnp.where(open_mask[None], raw, masked_score)

    def sweep(step, carry):

        def memory_turn(block, state):
            return step(
                state,
                block,
                memory_key_blocks[block],
                memory_value_blocks[block],
                memory_open,
                False,
            )

        def own_turn(block, state):
            return step(state, block, key_blocks[block], value_blocks[block], own_open(block), True)

        carry = lax.fori_loop(0, memory_blocks, memory_turn, carry)
        return lax.fori_loop(0, own_count, own_turn, carry)

    def max_step(carry, block, key_block, value_block, open_mask, own):
        row_max, row_sum = carry
        scores = block_scores(key_block, open_mask)
        new_max = jnp.maximum(row_max, jnp.max(scores, axis=2))
        row_sum = row_sum * jnp.exp(row_max - new_max) + jnp.sum(
            jnp.exp(scores - new_max[..., None]), axis=2
        )
        return (new_max, row_sum)

    start_max = jnp.full((HEADS, tokens), masked_score, jnp.float32)
    row_max, row_sum = sweep(max_step, (start_max, jnp.zeros((HEADS, tokens), jnp.float32)))
    log_totals = row_max + jnp.log(row_sum)

    def mix_step(total, block, key_block, value_block, open_mask, own):
        weights_low = jnp.exp(block_scores(key_block, open_mask) - log_totals[..., None]).astype(
            jnp.bfloat16
        )
        return total + jnp.einsum(
            "hqk,khd->qhd", weights_low, value_block, preferred_element_type=jnp.float32
        )

    attended = sweep(mix_step, jnp.zeros((tokens, HEADS, HEAD_DIM), jnp.float32))
    attended_low = attended.reshape(tokens, D).astype(jnp.bfloat16)
    residual = inputs + product(attended_low, w_out)
    second_norm, second_inverse = norm_forward(residual, norm2_gain)
    second_low = second_norm.astype(jnp.bfloat16)
    gate_values = product(second_low, w_gate)
    up_values = product(second_low, w_up)
    sigmoid_gate = jax.nn.sigmoid(gate_values)
    activated = gate_values * sigmoid_gate
    hidden_low = (activated * up_values).astype(jnp.bfloat16)
    output = (residual + product(hidden_low, w_down)).astype(jnp.bfloat16)
    upstream = output_grad[0]
    grad_down = product_tn(hidden_low, upstream)
    grad_hidden = product_nt(upstream, w_down)
    grad_gate_low = (
        grad_hidden * up_values * sigmoid_gate * (1.0 + gate_values * (1.0 - sigmoid_gate))
    ).astype(jnp.bfloat16)
    grad_up_low = (grad_hidden * activated).astype(jnp.bfloat16)
    grad_gate = product_tn(second_low, grad_gate_low)
    grad_up = product_tn(second_low, grad_up_low)
    grad_second = product_nt(grad_gate_low, w_gate) + product_nt(grad_up_low, w_up)
    grad_residual, grad_norm2 = norm_backward(residual, second_inverse, norm2_gain, grad_second)
    grad_residual = grad_residual + upstream.astype(jnp.float32)
    residual_low = grad_residual.astype(jnp.bfloat16)
    grad_out = product_tn(attended_low, residual_low)
    grad_attended = product_nt(residual_low, w_out).astype(jnp.bfloat16)
    grad_heads = grad_attended.reshape(tokens, HEADS, HEAD_DIM)

    def probs_pair(key_block, value_block, open_mask):
        probs = jnp.exp(block_scores(key_block, open_mask) - log_totals[..., None])
        dprobs = jnp.einsum(
            "qhd,khd->hqk", grad_heads, value_block, preferred_element_type=jnp.float32
        )
        return (probs, dprobs)

    def delta_step(total, block, key_block, value_block, open_mask, own):
        probs, dprobs = probs_pair(key_block, value_block, open_mask)
        return total + jnp.sum(probs * dprobs, axis=2)

    delta_rows = sweep(delta_step, jnp.zeros((HEADS, tokens), jnp.float32))

    def grad_step(carry, block, key_block, value_block, open_mask, own):
        grad_query, key_terms, value_terms = carry
        probs, dprobs = probs_pair(key_block, value_block, open_mask)
        dscores = (probs * (dprobs - delta_rows[..., None])).astype(jnp.bfloat16)
        grad_query = grad_query + jnp.einsum(
            "hqk,khd->qhd", dscores, key_block, preferred_element_type=jnp.float32
        )
        if own:
            key_part = (
                jnp.einsum("hqk,qhd->khd", dscores, query_heads, preferred_element_type=jnp.float32)
                * score_scale
            )
            value_part = jnp.einsum(
                "hqk,qhd->khd",
                probs.astype(jnp.bfloat16),
                grad_heads,
                preferred_element_type=jnp.float32,
            )
            key_terms = lax.dynamic_update_index_in_dim(key_terms, key_part, block, 0)
            value_terms = lax.dynamic_update_index_in_dim(value_terms, value_part, block, 0)
        return (grad_query, key_terms, value_terms)

    term_shape = key_blocks.shape
    start_grads = (
        jnp.zeros((tokens, HEADS, HEAD_DIM), jnp.float32),
        jnp.zeros(term_shape, jnp.float32),
        jnp.zeros(term_shape, jnp.float32),
    )
    grad_query, key_terms, value_terms = sweep(grad_step, start_grads)
    grad_queries = (grad_query * score_scale).reshape(tokens, D)
    grad_keys, grad_values = (
        lax.psum_scatter(
            key_terms.astype(jnp.bfloat16), "seq", scatter_dimension=0, tiled=True
        ).astype(jnp.float32),
        lax.psum_scatter(
            value_terms.astype(jnp.bfloat16), "seq", scatter_dimension=0, tiled=True
        ).astype(jnp.float32),
    )
    grad_projected = jnp.concatenate(
        [
            rotate(grad_queries, cosine_table, sine_table, -1.0),
            rotate(grad_keys.reshape(tokens, D), cosine_table, sine_table, -1.0),
            grad_values.reshape(tokens, D),
        ],
        axis=1,
    ).astype(jnp.bfloat16)
    grad_qkv = product_tn(first_low, grad_projected)
    grad_first = product_nt(grad_projected, w_qkv)
    grad_inputs, grad_norm1 = norm_backward(inputs, first_inverse, norm1_gain, grad_first)
    input_grad = (grad_inputs + grad_residual)[None]
    shares = (
        lax.psum_scatter(
            grad_norm1.astype(jnp.bfloat16), "seq", scatter_dimension=0, tiled=True
        ).astype(jnp.float32),
        lax.psum_scatter(
            grad_norm2.astype(jnp.bfloat16), "seq", scatter_dimension=0, tiled=True
        ).astype(jnp.float32),
        lax.psum_scatter(
            grad_qkv.astype(jnp.bfloat16), "seq", scatter_dimension=0, tiled=True
        ).astype(jnp.float32),
        lax.psum_scatter(
            grad_out.astype(jnp.bfloat16), "seq", scatter_dimension=0, tiled=True
        ).astype(jnp.float32),
        lax.psum_scatter(
            grad_gate.astype(jnp.bfloat16), "seq", scatter_dimension=0, tiled=True
        ).astype(jnp.float32),
        lax.psum_scatter(
            grad_up.astype(jnp.bfloat16), "seq", scatter_dimension=0, tiled=True
        ).astype(jnp.float32),
        lax.psum_scatter(
            grad_down.astype(jnp.bfloat16), "seq", scatter_dimension=0, tiled=True
        ).astype(jnp.float32),
    )
    totals = (
        lax.psum(shares[0].astype(jnp.bfloat16), "seg").astype(jnp.float32),
        lax.psum(shares[1].astype(jnp.bfloat16), "seg").astype(jnp.float32),
        lax.psum(shares[2].astype(jnp.bfloat16), "seg").astype(jnp.float32),
        lax.psum(shares[3].astype(jnp.bfloat16), "seg").astype(jnp.float32),
        lax.psum(shares[4].astype(jnp.bfloat16), "seg").astype(jnp.float32),
        lax.psum(shares[5].astype(jnp.bfloat16), "seg").astype(jnp.float32),
        lax.psum(shares[6].astype(jnp.bfloat16), "seg").astype(jnp.float32),
    )
    return (
        output[None],
        input_grad,
        totals[0],
        totals[1],
        totals[2],
        totals[3],
        totals[4],
        totals[5],
        totals[6],
    )


def solution(mesh):
    placed = (
        P("seg", "seq", None),
        P("seg", "seq", None),
        P(),
        P(),
        P(),
        P(),
        P(),
        P(),
        P(),
        P("seg", "seq", None),
        P("seg", "seq", None),
        P(),
        P(),
    )
    return jax.shard_map(
        on_device,
        mesh=mesh,
        in_specs=placed,
        out_specs=(
            P("seg", "seq", None),
            P("seg", "seq", None),
            P("seq"),
            P("seq"),
            P("seq", None),
            P("seq", None),
            P("seq", None),
            P("seq", None),
            P("seq", None),
        ),
        check_vma=False,
    )
```

profile of v0, /device:TPU:0, one launch (start us, length us, event | category | flops | bytes accessed | tf_op | source)
XLA Modules:
  0.0 1502.4 jit_solution(4767216906355732668)
XLA Ops:
  39.9 19.3 %all-gather.7.cloned.1.call-done = bf16[8,256,1024]{2,1,0:T(8,128)(2,1)} async-done(((bf16[1,256,1024]{2,1,0:T(8,128)(2,1)}), bf16[8,256,1024]{2,1,0:T(8,128)(2,1)}) %all-gather.7.cloned.1.call-update) | async-done | bytes 4194320 | tf_op jit(solution)/shard_map/all_gather | solution.py:87
  63.4 43.1 %all-gather.11.cloned.1.call-done = bf16[8,256,1024]{2,1,0:T(8,128)(2,1)} async-done(((bf16[1,256,1024]{2,1,0:T(8,128)(2,1)}), bf16[8,256,1024]{2,1,0:T(8,128)(2,1)}) %all-gather.11.cloned.1.call-update) | async-done | bytes 4194320 | tf_op jit(solution)/shard_map/all_gather | solution.py:86
  118.4 41.9 %all-gather.15.cloned.1.call-done = bf16[2048,1024]{1,0:T(8,128)(2,1)} async-done(((bf16[512,1024]{1,0:T(8,128)(2,1)}), bf16[2048,1024]{1,0:T(8,128)(2,1)}) %all-gather.15.cloned.1.call-update) | async-done | bytes 4194320 | tf_op jit(solution)/shard_map/all_gather | solution.py:108
  166.5 48.7 %all-gather.17.cloned.1.call-done = bf16[2048,1024]{1,0:T(8,128)(2,1)} async-done(((bf16[512,1024]{1,0:T(8,128)(2,1)}), bf16[2048,1024]{1,0:T(8,128)(2,1)}) %all-gather.17.cloned.1.call-update) | async-done | bytes 4194320 | tf_op jit(solution)/shard_map/all_gather | solution.py:109
  221.9 83.1 %all-gather.13.cloned.1.call-done = bf16[4,1024,1024]{2,1,0:T(8,128)(2,1)} async-done(((bf16[4,256,1024]{2,1,0:T(8,128)(2,1)}), bf16[4,1024,1024]{2,1,0:T(8,128)(2,1)}) %all-gather.13.cloned.1.call-update) | async-done | bytes 8388624 | tf_op jit(solution)/shard_map/all_gather | solution.py:92
  305.0 8.9 copy.127
  313.9 10.1 copy.87
  324.0 88.0 %while.112 = (s32[]{:T(128)}, f32[8,512]{1,0:T(8,128)S(1)}, f32[8,512]{1,0:T(8,128)S(1)}, bf16[8,512,8,128]{3,1,2,0:T(8,128)(2,1)}, bf16[512,8,128]{2,0,1:T(8,128)(2,1)S(1)}, /*index=5*/pred[]{:T(512)}, s32[]{:T(128)}, s32[]{:T(128)}) while((s32[]{:T(128)}, f32[8,512]{1,0:T(8,128)S(1)}, f32[8,512]{1,0:T(8,128)S(1)}, ...), condition=%wide.region_4.6_spmd.clone, body=%wide.region_1.5_spmd.clone.sunk | while | flops 551571456 | bytes 19088480 | solution.py:143
  416.8 8.9 copy.126
  425.7 9.1 copy.102
  434.8 85.3 %while.113 = (s32[]{:T(128)}, f32[512,8,128]{0,2,1:T(8,128)}, bf16[8,512,8,128]{3,2,1,0:T(8,128)(2,1)}, bf16[8,512,8,128]{3,1,2,0:T(8,128)(2,1)}, bf16[512,8,128...) while((s32[]{:T(128)}, f32[512,8,128]{0,2,1:T(8,128)}, ...), condition=%wide.region_10.12_spmd.clone, body=%wide.region_9.11_spmd.clone.sunk | while | flops 1083179008 | bytes 11551851 | solution.py:143
  520.2 11.2 while.109
  545.4 11.5 multiply_convert_fusion
  569.2 48.3 %while.114 = (s32[]{:T(128)}, f32[8,512]{1,0:T(8,128)S(1)}, bf16[8,512,8,128]{3,1,2,0:T(8,128)(2,1)}, bf16[512,8,128]{2,0,1:T(8,128)(2,1)S(1)}, f32[8,512]{1,0:T...) while((s32[]{:T(128)}, f32[8,512]{1,0:T(8,128)S(1)}, ...), condition=%wide.region_17.19_spmd.clone, body=%wide.region_15.18_spmd.clone.sunk | while | flops 1084231680 | bytes 21055084 | solution.py:143
  618.5 13.1 while.110
  631.6 106.0 %while.115 = (s32[]{:T(128)}, f32[512,8,128]{0,2,1:T(8,128)S(1)}, bf16[8,512,8,128]{3,1,2,0:T(8,128)(2,1)}, bf16[512,8,128]{2,0,1:T(8,128)(2,1)S(1)}, f32[8,512]...) while((s32[]{:T(128)}, f32[512,8,128]{0,2,1:T(8,128)S(1)}, ...), condition=%wide.region_22.24_spmd.clone, body=%wide.region_21.23_spmd.clone.sunk | while | flops 1624244224 | bytes 26249336 | solution.py:143
  637.3 7.5 bitcast_add_fusion.13
  677.1 7.5 bitcast_add_fusion.13
  743.4 22.3 %while.111 = (s32[]{:T(128)}, f32[512,8,128]{0,2,1:T(8,128)S(1)}, bf16[4,512,8,128]{3,1,2,0:T(8,128)(2,1)}, bf16[4,512,8,128]{3,1,2,0:T(8,128)(2,1)}, s32[]{:T(1...) while((s32[]{:T(128)}, f32[512,8,128]{0,2,1:T(8,128)S(1)}, ...), condition=%wide.region_24.26_spmd.clone, body=%wide.region_23.25_spmd.clone.sunk | while | flops 2706637824 | bytes 117236072 | solution.py:144
  771.5 7.8 convolution_convert_fusion.1
  802.1 168.8 %reduce-scatter.22.cloned.1.call-done = bf16[1,512,8,128]{3,1,2,0:T(8,128)(2,1)} async-done(((bf16[4,512,8,128]{3,1,2,0:T(8,128)(2,1)}), bf16[1,512,8,128]{3,1,2,0:T(8,128)(2,1)}) %reduce-scatter.22.cloned.1.call-update) | async-done | bytes 1048592
  978.9 47.6 %reduce-scatter.24.cloned.1.call-done = bf16[1,512,8,128]{3,1,2,0:T(8,128)(2,1)} async-done(((bf16[4,512,8,128]{3,1,2,0:T(8,128)(2,1)}), bf16[1,512,8,128]{3,1,2,0:T(8,128)(2,1)}) %reduce-scatter.24.cloned.1.call-update) | async-done | bytes 1048592
  1039.4 25.3 %reduce-scatter.14.cloned.1.call-done = bf16[256,1024]{1,0:T(8,128)(2,1)} async-done(((bf16[1024,1024]{1,0:T(8,128)(2,1)}), bf16[256,1024]{1,0:T(8,128)(2,1)}) %reduce-scatter.14.cloned.1.call-update) | async-done | bytes 524304 | tf_op jit(solution)/shard_map/reduce_scatter | solution.py:268
  1064.7 68.5 %reduce-scatter.18.cloned.1.call-done = bf16[256,2816]{1,0:T(8,128)(2,1)} async-done(((bf16[1024,2816]{1,0:T(8,128)(2,1)}), bf16[256,2816]{1,0:T(8,128)(2,1)}) %reduce-scatter.18.cloned.1.call-update) | async-done | bytes 1441808 | tf_op jit(solution)/shard_map/reduce_scatter | solution.py:274
  1133.2 68.7 %reduce-scatter.16.cloned.1.call-done = bf16[256,2816]{1,0:T(8,128)(2,1)} async-done(((bf16[1024,2816]{1,0:T(8,128)(2,1)}), bf16[256,2816]{1,0:T(8,128)(2,1)}) %reduce-scatter.16.cloned.1.call-update) | async-done | bytes 1441808 | tf_op jit(solution)/shard_map/reduce_scatter | solution.py:271
  1201.9 68.5 %reduce-scatter.20.cloned.1.call-done = bf16[704,1024]{1,0:T(8,128)(2,1)} async-done(((bf16[2816,1024]{1,0:T(8,128)(2,1)}), bf16[704,1024]{1,0:T(8,128)(2,1)}) %reduce-scatter.20.cloned.1.call-update) | async-done | bytes 1441808 | tf_op jit(solution)/shard_map/reduce_scatter | solution.py:277
  1270.5 73.0 %reduce-scatter.12.cloned.1.call-done = bf16[256,3072]{1,0:T(8,128)(2,1)} async-done(((bf16[1024,3072]{1,0:T(8,128)(2,1)}), bf16[256,3072]{1,0:T(8,128)(2,1)}) %reduce-scatter.12.cloned.1.call-update) | async-done | bytes 1572880 | tf_op jit(solution)/shard_map/reduce_scatter | solution.py:265
  1345.5 7.8 fusion.166
  1353.3 8.1 fusion.157
  1361.4 8.9 all-reduce.6
  1370.4 15.4 %all-reduce.4 = (bf16[256]{0:T(256)(128)(2,1)S(1)}, bf16[256]{0:T(256)(128)(2,1)S(1)}) all-reduce(bf16[256]{0:T(256)(128)(2,1)S(1)} %dynamic-slice.5, bf16[256]{0:T(256)(128)(2,1)S(1)} %dynamic-slice.7), channel_id=1, replica_groups=mesh['seg'=8,'seq'=4] {'seg'}, use_global_device_ids=true, to_apply=%region_30.32 | all-reduce | flops 512 | bytes 2048 | tf_op jit(solution)/shard_map/psum | solution.py:282
  1390.5 94.6 %all-reduce.9.cloned.1.call-done = (bf16[256,3072]{1,0:T(8,128)(2,1)}, bf16[256,1024]{1,0:T(8,128)(2,1)}, bf16[256,2816]{1,0:T(8,128)(2,1)}, bf16[256,2816]{1,0:T(8,128)(2,1)}, bf16[704,1024]{1,0:T(8,128)(2,1)}) async-done(((bf16[256,3072]{1,0:T(8,128)(2,1)}, bf16[256,1024]{1,0:T(8,128)(2,1)}, bf16[256,2816]{1,0:T(8,128)(2,1)}, bf16[256,2816]{1,0:T(8,128)(2,1)}, bf16[704,1024]{1,0:T(8,128)(2,1)}), ...) | async-done | bytes 6422544 | tf_op jit(solution)/shard_map/psum | solution.py:284
  (352 shorter events, 525.9 us)
Async XLA Ops:
  7.2 526.1 %copy-start = (bf16[1024,1024]{1,0:T(8,128)(2,1)S(1)}, bf16[1024,1024]{1,0:T(8,128)(2,1)}, u32[]{:S(2)}) copy-start(bf16[1024,1024]{1,0:T(8,128)(2,1)} %param.36) | copy-start | bytes 6291460
  7.2 52.0 %all-gather.7.cloned.1.call-start = ((), (), s32[]{:S(2)}) async-start(), calls=%async_computation.7 | async-start | bytes 4718592 | tf_op jit(solution)/shard_map/all_gather | solution.py:87
  7.9 98.6 %all-gather.11.cloned.1.call-start = ((), (), s32[]{:S(2)}) async-start(), calls=%async_computation.9 | async-start | bytes 4718592 | tf_op jit(solution)/shard_map/all_gather | solution.py:86
  8.7 151.7 %all-gather.15.cloned.1.call-start = ((), (), s32[]{:S(2)}) async-start(), calls=%async_computation.11 | async-start | bytes 5242880 | tf_op jit(solution)/shard_map/all_gather | solution.py:108
  10.8 6.0 copy-start.43
  31.3 5.4 copy-start.7
  36.7 178.5 %all-gather.17.cloned.1.call-start = ((), (), s32[]{:S(2)}) async-start(), calls=%async_computation.12 | async-start | bytes 5242880 | tf_op jit(solution)/shard_map/all_gather | solution.py:109
  39.6 265.4 %all-gather.13.cloned.1.call-start = ((), (), s32[]{:S(2)}) async-start(), calls=%async_computation.10 | async-start | bytes 10485760 | tf_op jit(solution)/shard_map/all_gather | solution.py:92
  115.4 301.4 %all-gather.9.cloned.1.call-start = ((), (), s32[]{:S(2)}) async-start(), calls=%async_computation.8 | async-start | bytes 10485760 | tf_op jit(solution)/shard_map/all_gather | solution.py:93
  221.8 749.1 %reduce-scatter.22.cloned.1.call-start = ((), (), s32[]{:S(2)}) async-start(), calls=%async_computation.18 | async-start | bytes 5242880
  533.3 7.2 slice-start.6
  534.7 32.3 %copy-start.4 = (f32[512,1024]{1,0:T(8,128)}, f32[512,1024]{1,0:T(8,128)S(1)}, u32[]{:S(2)}) copy-start(f32[512,1024]{1,0:T(8,128)S(1)} %get-tuple-element.1348) | copy-start | bytes 6291460
  535.5 5.0 copy-start.32
  535.5 5.0 slice-start.7
  556.9 6.0 copy-start.50
  618.5 13.1 copy-start.2
  749.6 6.7 copy-start.9
  756.3 6.3 slice-start
  765.8 260.7 %reduce-scatter.24.cloned.1.call-start = ((), (), s32[]{:S(2)}) async-start(), calls=%async_computation.19 | async-start | bytes 5242880
  766.5 298.2 %reduce-scatter.14.cloned.1.call-start = ((), (), s32[]{:S(2)}) async-start(), calls=%async_computation.14 | async-start | bytes 2621440 | tf_op jit(solution)/shard_map/reduce_scatter | solution.py:268
  771.2 362.0 %reduce-scatter.18.cloned.1.call-start = ((), (), s32[]{:S(2)}) async-start(), calls=%async_computation.16 | async-start | bytes 7208960 | tf_op jit(solution)/shard_map/reduce_scatter | solution.py:274
  779.4 422.6 %reduce-scatter.16.cloned.1.call-start = ((), (), s32[]{:S(2)}) async-start(), calls=%async_computation.15 | async-start | bytes 7208960 | tf_op jit(solution)/shard_map/reduce_scatter | solution.py:271
  787.4 483.1 %reduce-scatter.20.cloned.1.call-start = ((), (), s32[]{:S(2)}) async-start(), calls=%async_computation.17 | async-start | bytes 7208960 | tf_op jit(solution)/shard_map/reduce_scatter | solution.py:277
  795.5 548.1 %reduce-scatter.12.cloned.1.call-start = ((), (), s32[]{:S(2)}) async-start(), calls=%async_computation.13 | async-start | bytes 7864320 | tf_op jit(solution)/shard_map/reduce_scatter | solution.py:265
  977.6 51.1 %copy-start.19 = (bf16[1,512,8,128]{3,1,2,0:T(8,128)(2,1)S(1)}, bf16[1,512,8,128]{3,1,2,0:T(8,128)(2,1)}, u32[]{:S(2)}) copy-start(bf16[1,512,8,128]{3,1,2,0:T(8,128)(2,1)} %reduce-scatter.22.cloned.1.call-done) | copy-start | bytes 3145732
  1039.1 446.0 %all-reduce.9.cloned.1.call-start = ((), (), s32[]{:S(2)}) async-start(), calls=%async_computation.20 | async-start | bytes 12845056 | tf_op jit(solution)/shard_map/psum | solution.py:284
  1345.4 7.8 copy-start.31
  1345.4 7.8 copy-start.37
  1345.5 7.8 copy-start.39
  1353.2 8.1 copy-start.47
  1353.3 33.7 %copy-start.15 = (f32[512,1024]{1,0:T(8,128)S(1)}, f32[512,1024]{1,0:T(8,128)}, u32[]{:S(2)}) copy-start(f32[512,1024]{1,0:T(8,128)} %copy-done.14) | copy-start | bytes 6291460
  1353.3 33.7 %copy-start.42 = (f32[512]{0:T(512)S(1)}, f32[512]{0:T(512)}, u32[]{:S(2)}) copy-start(f32[512]{0:T(512)} %get-tuple-element.1341) | copy-start | bytes 6148
  (41 other events, 92.3 us)
Sparse Core Ops, SparseCore 0:
  9.6 49.5 all-gather.6
  60.8 45.6 all-gather.10
  109.0 51.3 all-gather.14
  162.6 52.5 all-gather.16
  217.5 87.4 all-gather.12
  307.3 87.4 all-gather.8
  765.9 204.9 reduce-scatter.21
  973.8 52.5 reduce-scatter.23
  1029.5 35.1 reduce-scatter.13
  1067.5 65.6 reduce-scatter.17
  1136.2 65.6 reduce-scatter.15
  1204.8 65.6 reduce-scatter.19
  1273.5 70.0 reduce-scatter.11
  1346.1 138.8 all-reduce.8
where the time goes:
time: 1510 us; the launch traced here: 1500 us
  waiting for transfers between devices  854 us (57%)
  matrix products  377 us (25%)
  local copies, waits for them, and re-layouts  138 us (9%)
  other arithmetic  89.1 us (6%)
  blocking collectives  24.3 us (2%)
  between operations  16.4 us (1%)
    unnamed x16, waiting for transfers between devices  219 us
    dot_general x27, matrix products, block_scores(): jnp.einsum('qhd,khd->hqk', query_heads, key_block, preferred_element_type...  127 us
    psum x1, waiting for transfers between devices, on_device(): lax.psum(shares[2].astype(jnp.bfloat16), 'seg').astype(jnp.float32)  94.6 us
    all_gather x1, waiting for transfers between devices, on_device(): lax.all_gather(chosen_keys, 'seq', axis=1, tiled=True)  83.1 us
    reduce_scatter x1, waiting for transfers between devices, on_device(): lax.psum_scatter(grad_qkv.astype(jnp.bfloat16), 'seq', scatter_dimension=...  73 us
    unnamed x123, local copies, waits for them, and re-layouts  69.1 us
    reduce_scatter x1, waiting for transfers between devices, on_device(): lax.psum_scatter(grad_gate.astype(jnp.bfloat16), 'seq', scatter_dimension...  68.7 us
    reduce_scatter x1, waiting for transfers between devices, on_device(): lax.psum_scatter(grad_down.astype(jnp.bfloat16), 'seq', scatter_dimension...  68.5 us
  transfers between devices with their start and end apart: 14, of which 13 were waited for; matrix products, arithmetic and copies ran while one was open for 16% of the time, Pallas kernels for 0%

commit v1 on v0

--- a/solution.py
+++ b/solution.py
@@ -1,6 +1,11 @@
+import functools
+import math
+
 import jax
 import jax.numpy as jnp
 from jax import lax
+from jax.experimental import pallas as pl
+from jax.experimental.pallas import tpu as pltpu
 from jax.sharding import PartitionSpec as P
 
 D = 1024
@@ -60,7 +65,7 @@
     )
 
 
-def on_device(
+def general_plan(
     layer_input,
     output_grad,
     norm1_gain,
@@ -300,7 +305,405 @@
     )
 
 
+VMEM_BYTES = 60 * 1024 * 1024
+LN2 = math.log(2.0)
+SCORE_SCALE = HEAD_DIM ** (-0.5)
+
+
+def lane_fold(op, tile, running):
+    for column in range(tile.shape[1] // HEAD_DIM):
+        piece = tile[:, column * HEAD_DIM : (column + 1) * HEAD_DIM]
+        running = piece if running is None else op(running, piece)
+    return running
+
+
+def causal(scores):
+    rows = lax.broadcasted_iota(jnp.int32, scores.shape, 0)
+    columns = lax.broadcasted_iota(jnp.int32, scores.shape, 1)
+    return jnp.where(columns <= rows, scores, masked_score)
+
+
+def attend(query, pairs, diagonal, carried):
+    every, lane_max = [], None
+    for index, (keys, _) in enumerate(pairs):
+        scores = product_nt(query, keys)
+        if diagonal and index == len(pairs) - 1:
+            scores = causal(scores)
+        lane_max = lane_fold(jnp.maximum, scores, lane_max)
+        every.append(scores)
+    row_max = jnp.max(lane_max, axis=1, keepdims=True)
+    if carried is not None:
+        row_max = jnp.maximum(row_max, carried[0])
+    lane_sum, mixed = None, None
+    for scores, (_, values) in zip(every, pairs):
+        probs = jnp.exp2(scores - row_max)
+        lane_sum = lane_fold(jnp.add, probs, lane_sum)
+        part = product(probs.astype(jnp.bfloat16), values)
+        mixed = part if mixed is None else mixed + part
+    row_sum = jnp.sum(lane_sum, axis=1, keepdims=True)
+    if carried is not None:
+        shrink = jnp.exp2(carried[0] - row_max)
+        row_sum = carried[1] * shrink + row_sum
+        mixed = carried[2] * shrink + mixed
+    return row_max, row_sum, mixed
+
+
+def own_forward_kernel(rows, count, q_ref, k_ref, v_ref, mix_ref, max_ref, sum_ref):
+    block = pl.program_id(1)
+    for index in range(count):
+
+        @pl.when(block == index)
+        def _(index=index):
+            pairs = [
+                (k_ref[n * rows : (n + 1) * rows, :], v_ref[n * rows : (n + 1) * rows, :])
+                for n in range(index + 1)
+            ]
+            row_max, row_sum, mixed = attend(q_ref[...], pairs, True, None)
+            mix_ref[...] = mixed
+            max_ref[...] = jnp.broadcast_to(row_max, max_ref.shape)
+            sum_ref[...] = jnp.broadcast_to(row_sum, sum_ref.shape)
+
+
+def own_forward(queries, keys, values, rows=512):
+    length, width = queries.shape
+    block = pl.BlockSpec((rows, HEAD_DIM), lambda h, i: (i, h))
+    whole = pl.BlockSpec((length, HEAD_DIM), lambda h, i: (0, h))
+    heads = width // HEAD_DIM
+    pairs = heads * length * length // 2
+    return pl.pallas_call(
+        functools.partial(own_forward_kernel, rows, length // rows),
+        grid=(heads, length // rows),
+        in_specs=[block, whole, whole],
+        out_specs=[block] * 3,
+        out_shape=[jax.ShapeDtypeStruct((length, width), jnp.float32)] * 3,
+        compiler_params=pltpu.CompilerParams(vmem_limit_bytes=VMEM_BYTES),
+        cost_estimate=pl.CostEstimate(
+            flops=8 * pairs * HEAD_DIM, transcendentals=pairs, bytes_accessed=18 * length * width
+        ),
+        name="own_forward",
+    )(queries, keys, values)
+
+
+def memory_specs(heads, rows, count):
+    specs = []
+    for slot in range(count):
+        specs.append(
+            pl.BlockSpec((1, rows, HEAD_DIM), lambda h, i, chosen, slot=slot: (chosen[slot], 0, h))
+        )
+        specs.append(
+            pl.BlockSpec(
+                (1, rows, HEAD_DIM), lambda h, i, chosen, slot=slot: (chosen[slot], 0, heads + h)
+            )
+        )
+    return specs
+
+
+def memory_forward_kernel(count, chosen, q_ref, mix_ref, max_ref, sum_ref, *rest):
+    blocks = rest[: 2 * count]
+    low_ref, out_ref, log_ref = rest[2 * count :]
+    carried = (max_ref[:, :1], sum_ref[:, :1], mix_ref[...])
+
+    def finish(row_max, row_sum, mixed):
+        out = mixed * (1.0 / row_sum)
+        out_ref[...] = out
+        low_ref[...] = out.astype(jnp.bfloat16)
+        log_ref[...] = jnp.broadcast_to(row_max + jnp.log2(row_sum), log_ref.shape)
+
+    @pl.when(chosen[count] > 0)
+    def _():
+        pairs = [(blocks[2 * n][0], blocks[2 * n + 1][0]) for n in range(count)]
+        finish(*attend(q_ref[...], pairs, False, carried))
+
+    @pl.when(chosen[count] <= 0)
+    def _():
+        finish(*carried)
+
+
+def memory_forward(chosen, queries, mixed, row_max, row_sum, memory, rows=512):
+    length, width = queries.shape
+    heads, count = width // HEAD_DIM, chosen.shape[0] - 1
+    block = pl.BlockSpec((rows, HEAD_DIM), lambda h, i, chosen: (i, h))
+    pairs = heads * length * count * memory.shape[1]
+    return pl.pallas_call(
+        functools.partial(memory_forward_kernel, count),
+        grid_spec=pltpu.PrefetchScalarGridSpec(
+            num_scalar_prefetch=1,
+            grid=(heads, length // rows),
+            in_specs=[block] * 4 + memory_specs(heads, memory.shape[1], count),
+            out_specs=[block] * 3,
+        ),
+        out_shape=[
+            jax.ShapeDtypeStruct((length, width), jnp.bfloat16),
+            jax.ShapeDtypeStruct((length, width), jnp.float32),
+            jax.ShapeDtypeStruct((length, width), jnp.float32),
+        ],
+        compiler_params=pltpu.CompilerParams(vmem_limit_bytes=VMEM_BYTES),
+        cost_estimate=pl.CostEstimate(
+            flops=8 * pairs * HEAD_DIM, transcendentals=pairs, bytes_accessed=36 * length * width
+        ),
+        name="memory_forward",
+    )(chosen, queries, mixed, row_max, row_sum, *[memory] * (2 * count))
+
+
+def memory_backward_kernel(count, tile, chosen, q_ref, g_ref, out_ref, log_ref, *rest):
+    blocks = rest[: 2 * count]
+    dq_ref, delta_ref = rest[2 * count :]
+    query, upstream = q_ref[...], g_ref[...]
+    delta = jnp.sum(upstream.astype(jnp.float32) * out_ref[...], axis=1, keepdims=True)
+    delta_ref[...] = jnp.broadcast_to(delta, delta_ref.shape)
+    log_total = log_ref[:, :1]
+
+    @pl.when(chosen[count] > 0)
+    def _():
+        total = jnp.zeros(dq_ref.shape, jnp.float32)
+        for n in range(count):
+            for start in range(0, blocks[0].shape[1], tile):
+                keys = blocks[2 * n][0, start : start + tile, :]
+                values = blocks[2 * n + 1][0, start : start + tile, :]
+                probs = jnp.exp2(product_nt(query, keys) - log_total)
+                dscores = probs * (product_nt(upstream, values) - delta)
+                total = total + product(dscores.astype(jnp.bfloat16), keys)
+        dq_ref[...] = total
+
+    @pl.when(chosen[count] <= 0)
+    def _():
+        dq_ref[...] = jnp.zeros(dq_ref.shape, jnp.float32)
+
+
+def memory_backward(chosen, queries, upstream, out, log_totals, memory, rows=512, tile=512):
+    length, width = queries.shape
+    heads, count = width // HEAD_DIM, chosen.shape[0] - 1
+    block = pl.BlockSpec((rows, HEAD_DIM), lambda h, i, chosen: (i, h))
+    pairs = heads * length * count * memory.shape[1]
+    return pl.pallas_call(
+        functools.partial(memory_backward_kernel, count, math.gcd(tile, memory.shape[1])),
+        grid_spec=pltpu.PrefetchScalarGridSpec(
+            num_scalar_prefetch=1,
+            grid=(heads, length // rows),
+            in_specs=[block] * 4 + memory_specs(heads, memory.shape[1], count),
+            out_specs=[block] * 2,
+        ),
+        out_shape=[jax.ShapeDtypeStruct((length, width), jnp.float32)] * 2,
+        compiler_params=pltpu.CompilerParams(vmem_limit_bytes=VMEM_BYTES),
+        cost_estimate=pl.CostEstimate(
+            flops=12 * pairs * HEAD_DIM, transcendentals=pairs, bytes_accessed=36 * length * width
+        ),
+        name="memory_backward",
+    )(chosen, queries, upstream, out, log_totals, *[memory] * (2 * count))
+
+
+def own_backward_kernel(
+    rows, q_ref, k_ref, v_ref, g_ref, log_ref, delta_ref, start_ref, dq_ref, dk_ref, dv_ref, dk, dv
+):
+    block = pl.program_id(1)
+
+    @pl.when(block == 0)
+    def _():
+        dk[...] = jnp.zeros_like(dk)
+        dv[...] = jnp.zeros_like(dv)
+
+    query, upstream = q_ref[...], g_ref[...]
+    log_total, delta = log_ref[:, :1], delta_ref[:, :1]
+
+    def turn(other, total, diagonal):
+        span = pl.ds(pl.multiple_of(other * rows, rows), rows)
+        keys = k_ref[span, :]
+        scores = product_nt(query, keys)
+        if diagonal:
+            scores = causal(scores)
+        probs = jnp.exp2(scores - log_total)
+        dscores = (probs * (product_nt(upstream, v_ref[span, :]) - delta)).astype(jnp.bfloat16)
+        dv[span, :] += product_tn(probs.astype(jnp.bfloat16), upstream)
+        dk[span, :] += product_tn(dscores, query)
+        return total + product(dscores, keys)
+
+    total = turn(block, start_ref[...], True)
+    total = lax.fori_loop(0, block, lambda other, total: turn(other, total, False), total)
+    dq_ref[...] = total * SCORE_SCALE
+
+    @pl.when(block == pl.num_programs(1) - 1)
+    def _():
+        dk_ref[...] = dk[...] * LN2
+        dv_ref[...] = dv[...]
+
+
+def own_backward(queries, keys, values, upstream, log_totals, delta, start, rows=512):
+    length, width = queries.shape
+    block = pl.BlockSpec((rows, HEAD_DIM), lambda h, i: (i, h))
+    whole = pl.BlockSpec((length, HEAD_DIM), lambda h, i: (0, h))
+    heads = width // HEAD_DIM
+    pairs = heads * length * length // 2
+    return pl.pallas_call(
+        functools.partial(own_backward_kernel, rows),
+        grid=(heads, length // rows),
+        in_specs=[block, whole, whole, block, block, block, block],
+        out_specs=[block, whole, whole],
+        out_shape=[jax.ShapeDtypeStruct((length, width), jnp.float32)] * 3,
+        scratch_shapes=[pltpu.VMEM((length, HEAD_DIM), jnp.float32)] * 2,
+        compiler_params=pltpu.CompilerParams(vmem_limit_bytes=VMEM_BYTES),
+        cost_estimate=pl.CostEstimate(
+            flops=20 * pairs * HEAD_DIM, transcendentals=pairs, bytes_accessed=36 * length * width
+        ),
+        name="own_backward",
+    )(queries, keys, values, upstream, log_totals, delta, start)
+
+
+def rotate_block(matrix, cosine_table, sine_table, direction):
+    row_count, width = matrix.shape
+    half_dim = HEAD_DIM // 2
+    shaped = matrix.reshape(row_count, width // HEAD_DIM, HEAD_DIM)
+    turned = jnp.concatenate([-shaped[..., half_dim:], shaped[..., :half_dim]], axis=-1)
+    return (shaped * cosine_table + direction * turned * sine_table).reshape(row_count, width)
+
+
+def core_groups(seg_size):
+    return [[2 * z, 2 * z + 1] for z in range(seg_size // 2)]
+
+
+def line_groups(seg_size):
+    return [[2 * z + core for z in range(seg_size // 2)] for core in range(2)]
+
+
+def reduce_rows(terms, seg_size, seq_size):
+    rows, columns = terms.shape
+    split = terms.astype(jnp.bfloat16).reshape(seq_size, 2, rows // (2 * seq_size), columns)
+    halves = jnp.swapaxes(split, 0, 1)
+    swapped = lax.all_to_all(halves, "seg", 0, 0, axis_index_groups=core_groups(seg_size))
+    chip = (swapped[0].astype(jnp.float32) + swapped[1].astype(jnp.float32)).astype(jnp.bfloat16)
+    share = lax.psum_scatter(chip, "seq", scatter_dimension=0)
+    total = lax.psum(share, "seg", axis_index_groups=line_groups(seg_size))
+    both = lax.all_gather(total, "seg", axis=0, axis_index_groups=core_groups(seg_size))
+    return both.reshape(rows // seq_size, columns).astype(jnp.float32)
+
+
+def head_plan(
+    seg_size,
+    seq_size,
+    layer_input,
+    output_grad,
+    norm1_gain,
+    norm2_gain,
+    w_qkv,
+    w_out,
+    w_gate,
+    w_up,
+    w_down,
+    mem_keys,
+    mem_values,
+    memory_flags,
+    sources,
+):
+    seg_index = lax.axis_index("seg")
+    seq_index = lax.axis_index("seq")
+    tokens = layer_input.shape[1]
+    length = tokens * seq_size
+    width = D // seq_size
+    flag = lax.dynamic_index_in_dim(memory_flags, seg_index, 0, keepdims=True)
+    listed = lax.dynamic_index_in_dim(sources, seg_index, 0, keepdims=False)
+    chosen = jnp.concatenate([jnp.reshape(seg_index, (1,)), listed, flag]).astype(jnp.int32)
+
+    mem_rows = mem_keys.shape[1]
+    both = jnp.concatenate(
+        [mem_keys[0].reshape(mem_rows, seq_size, width), mem_values[0].reshape(mem_rows, seq_size, width)],
+        axis=2,
+    ).reshape(mem_rows, 2 * D)
+    own_memory = lax.all_to_all(both, "seq", 1, 0, tiled=True)
+    memory = lax.all_gather(own_memory, "seg", axis=0)
+
+    inputs = layer_input[0].astype(jnp.float32)
+    first_norm, first_inverse = norm_forward(inputs, norm1_gain)
+    first_low = first_norm.astype(jnp.bfloat16)
+    every_low = lax.all_gather(first_low, "seq", axis=0, tiled=True)
+    w_heads = lax.dynamic_index_in_dim(
+        w_qkv.reshape(D, 3, seq_size, width), seq_index, 2, keepdims=False
+    ).reshape(D, 3 * width)
+    projected = product(every_low, w_heads)
+    cosine_table, sine_table = turn_tables(lax.iota(jnp.int32, length).astype(jnp.float32))
+    scale = SCORE_SCALE / LN2
+    queries = rotate_block(
+        projected[:, :width], cosine_table * scale, sine_table * scale, 1.0
+    ).astype(jnp.bfloat16)
+    keys = rotate_block(projected[:, width : 2 * width], cosine_table, sine_table, 1.0).astype(
+        jnp.bfloat16
+    )
+    values = projected[:, 2 * width :].astype(jnp.bfloat16)
+
+    mixed, row_max, row_sum = own_forward(queries, keys, values)
+    heads_low, heads_out, log_totals = memory_forward(
+        chosen, queries, mixed, row_max, row_sum, memory
+    )
+    attended_low = lax.all_to_all(heads_low, "seq", 0, 1, tiled=True)
+
+    residual = inputs + product(attended_low, w_out)
+    second_norm, second_inverse = norm_forward(residual, norm2_gain)
+    second_low = second_norm.astype(jnp.bfloat16)
+    gate_values = product(second_low, w_gate)
+    up_values = product(second_low, w_up)
+    sigmoid_gate = jax.nn.sigmoid(gate_values)
+    activated = gate_values * sigmoid_gate
+    hidden_low = (activated * up_values).astype(jnp.bfloat16)
+    output = (residual + product(hidden_low, w_down)).astype(jnp.bfloat16)
+    upstream = output_grad[0]
+    grad_down = reduce_rows(product_tn(hidden_low, upstream), seg_size, seq_size)
+    grad_hidden = product_nt(upstream, w_down)
+    grad_gate_low = (
+        grad_hidden * up_values * sigmoid_gate * (1.0 + gate_values * (1.0 - sigmoid_gate))
+    ).astype(jnp.bfloat16)
+    grad_up_low = (grad_hidden * activated).astype(jnp.bfloat16)
+    grad_gate = reduce_rows(product_tn(second_low, grad_gate_low), seg_size, seq_size)
+    grad_up = reduce_rows(product_tn(second_low, grad_up_low), seg_size, seq_size)
+    grad_second = product_nt(grad_gate_low, w_gate) + product_nt(grad_up_low, w_up)
+    grad_residual, grad_norm2 = norm_backward(residual, second_inverse, norm2_gain, grad_second)
+    grad_residual = grad_residual + upstream.astype(jnp.float32)
+    residual_low = grad_residual.astype(jnp.bfloat16)
+    grad_out = reduce_rows(product_tn(attended_low, residual_low), seg_size, seq_size)
+    grad_attended = product_nt(residual_low, w_out).astype(jnp.bfloat16)
+    grad_heads = lax.all_to_all(grad_attended, "seq", 1, 0, tiled=True)
+
+    start, delta = memory_backward(chosen, queries, grad_heads, heads_out, log_totals, memory)
+    grad_queries, grad_keys, grad_values = own_backward(
+        queries, keys, values, grad_heads, log_totals, delta, start
+    )
+    grad_projected = jnp.concatenate(
+        [
+            rotate_block(grad_queries, cosine_table, sine_table, -1.0),
+            rotate_block(grad_keys, cosine_table, sine_table, -1.0),
+            grad_values,
+        ],
+        axis=1,
+    ).astype(jnp.bfloat16)
+    part_first = product_nt(grad_projected, w_heads).astype(jnp.bfloat16)
+    grad_first = lax.psum_scatter(part_first, "seq", scatter_dimension=0, tiled=True).astype(
+        jnp.float32
+    )
+    part_qkv = product_tn(every_low, grad_projected).astype(jnp.bfloat16)
+    traded = lax.all_to_all(part_qkv.reshape(seq_size, D // seq_size, 3 * width), "seq", 0, 0)
+    rows_qkv = jnp.transpose(
+        traded.reshape(seq_size, D // seq_size, 3, width), (1, 2, 0, 3)
+    ).reshape(D // seq_size, 3 * D)
+    grad_qkv = lax.psum(rows_qkv, "seg").astype(jnp.float32)
+    grad_inputs, grad_norm1 = norm_backward(inputs, first_inverse, norm1_gain, grad_first)
+    input_grad = (grad_inputs + grad_residual)[None]
+    gains = jnp.stack([grad_norm1, grad_norm2], axis=0)
+    gain_total = lax.psum(gains, ("seg", "seq"))
+    gain_rows = lax.dynamic_slice_in_dim(gain_total, seq_index * width, width, 1)
+    return (
+        output[None],
+        input_grad,
+        gain_rows[0],
+        gain_rows[1],
+        grad_qkv,
+        grad_out,
+        grad_gate,
+        grad_up,
+        grad_down,
+    )
+
+
 def solution(mesh):
+    seq_size = mesh.shape["seq"]
+    heads_fit = HEADS % seq_size == 0 and mesh.shape["seg"] % 2 == 0
+    plan = functools.partial(head_plan, mesh.shape["seg"], seq_size) if heads_fit else general_plan
     placed = (
         P("seg", "seq", None),
         P("seg", "seq", None),
@@ -317,7 +720,7 @@
         P(),
     )
     return jax.shard_map(
-        on_device,
+        plan,
         mesh=mesh,
         in_specs=placed,
         out_specs=(

time: 1510 us -> 713 us (0.47)
  waiting for transfers between devices: 854 us -> 243 us
  matrix products: 377 us -> 76.9 us
  blocking collectives: 24.3 us -> 137 us
  Pallas kernels: 0 us -> 107 us
  local copies, waits for them, and re-layouts: 138 us -> 46.2 us
  other arithmetic: 89.1 us -> 72.9 us
    dot_general x57 -> x0, matrix products: 289 us -> none  [the longest x27 127 us: block_scores(): jnp.einsum('qhd,khd->hqk', query_heads, key_block, preferred_element_type...]
    reduce_scatter x5 -> x1, waiting for transfers between devices: 304 us -> 48.3 us  [head_plan(): lax.psum_scatter(part_first, 'seq', scatter_dimension=0, tiled=True)]
    unnamed x16, waiting for transfers between devices: 219 us -> 24.3 us
    all_gather x6 -> x5, waiting for transfers between devices: 236 us -> 46.7 us  [the longest x1 33 us: head_plan(): memory = lax.all_gather(own_memory, 'seg', axis=0)]
    pallas_call x0 -> x4, Pallas kernels: none -> 107 us  [the longest x1 34.9 us: memory_backward(): pl.pallas_call(functools.partial(memory_backward_kernel, count, math.gcd(...]
    all_to_all x0 -> x7, blocking collectives: none -> 95.7 us  [the longest x4 31.8 us: reduce_rows(): lax.all_to_all(halves, 'seg', 0, 0, axis_index_groups=core_groups(seg_size))]
    unnamed x123 -> x86, local copies, waits for them, and re-layouts: 69.1 us -> 15.5 us
    reduce_sum x9 -> x1, other arithmetic: 42.2 us -> 2.18 us  [norm_backward(): grad_gain = jnp.sum(upstream * values * inverse, axis=0)]
  transfers between devices with their start and end apart: 14 -> 13, of which waited for: 13 -> 7; matrix products, arithmetic and copies ran while one was open for 16% -> 21% of each run, Pallas kernels for 0% -> 11%
where the time goes in v1:
time: 713 us; the launch traced here: 702 us
  waiting for transfers between devices  243 us (34%)
  blocking collectives  137 us (19%)
  Pallas kernels  107 us (15%)
  matrix products  76.9 us (11%)
  other arithmetic  72.9 us (10%)
  local copies, waits for them, and re-layouts  46.2 us (6%)
  between operations  15.1 us (2%)
    psum x1, waiting for transfers between devices, reduce_rows(): total = lax.psum(share, 'seg', axis_index_groups=line_groups(seg_size))  60.1 us
    psum x1, waiting for transfers between devices, head_plan(): grad_qkv = lax.psum(rows_qkv, 'seg').astype(jnp.float32)  55.2 us
    reduce_scatter x1, waiting for transfers between devices, head_plan(): lax.psum_scatter(part_first, 'seq', scatter_dimension=0, tiled=True)  48.3 us
    psum x1, blocking collectives, head_plan(): gain_total = lax.psum(gains, ('seg', 'seq'))  39.4 us
    pallas_call x1, Pallas kernels, memory_backward(): pl.pallas_call(functools.partial(memory_backward_kernel, count, math.gcd(...  34.9 us
    all_gather x1, waiting for transfers between devices, head_plan(): memory = lax.all_gather(own_memory, 'seg', axis=0)  33 us
    all_to_all x4, blocking collectives, reduce_rows(): lax.all_to_all(halves, 'seg', 0, 0, axis_index_groups=core_groups(seg_size))  31.8 us
    pallas_call x1, Pallas kernels, memory_forward(): pl.pallas_call(functools.partial(memory_forward_kernel, count), grid_spec...  31.1 us
  transfers between devices with their start and end apart: 13, of which 7 were waited for; matrix products, arithmetic and copies ran while one was open for 21% of the time, Pallas kernels for 11%

profile of v1, /device:TPU:0, one launch (start us, length us, event | category | flops | bytes accessed | tf_op | source)
XLA Modules:
  0.0 702.1 jit_solution(10622911891163670651)
XLA Ops:
  14.8 27.5 %all_to_all.76 = bf16[256,4,512]{2,0,1:T(8,128)(2,1)} all-to-all(bf16[256,4,512]{2,0,1:T(8,128)(2,1)S(1)} %pad_maximum_fusion.4), channel_id=1, replica_groups=mesh['seg'=8,'seq'=4] {'seq'}, dimensions={1} | all-to-all | bytes 2097152 | tf_op jit(solution)/shard_map/all_to_all | solution.py:610
  43.1 8.7 %copy.48 = bf16[1024,3072]{0,1:T(8,128)(2,1)} copy(bf16[1024,3072]{1,0:T(8,128)(2,1)} %param.17) | data formatting | bytes 12582912 | tf_op args[4]
  56.2 5.4 broadcast_multiply_fusion
  61.6 13.6 %all-gather.6.cloned.1.call-done = bf16[2048,1024]{1,0:T(8,128)(2,1)} async-done(((bf16[512,1024]{1,0:T(8,128)(2,1)}), bf16[2048,1024]{1,0:T(8,128)(2,1)}) %all-gather.6.cloned.1.call-update) | async-done | bytes 4194320 | tf_op jit(solution)/shard_map/all_gather | solution.py:616
  75.3 5.7 fusion.32
  99.1 6.2 maximum_multiply_fusion
  109.4 16.5 %own_forward.1 = (f32[2048,256]{1,0:T(8,128)}, f32[2048,256]{1,0:T(8,128)}, f32[2048,256]{1,0:T(8,128)}) custom-call(bf16[2048,256]{1,0:T(8,128)(2,1)} %get-tuple-element.61.q_ref, bf16[2048,256]{1,0:T(8,128)(2,1)} %get-tuple-element.60.k_ref, bf16[2048,256]{1,0:T(8,128)(2,1)} %slice.119.v_ref), custom_call_target="tpu_custom_call" | custom-call | flops 4294967296 | bytes 9437184 | tf_op jit(solution)/shard_map/own_forward/pallas_call | solution.py:373
  125.9 33.0 %all-gather.8.cloned.1.call-done.rest_0_.rest_1_.rest_2_.rest_3_.rest_4_.rest_5_.rest_6_.rest_7_ = bf16[8,1024,512]{2,1,0:T(8,128)(2,1)} async-done(((bf16[1,1024,512]{2,1,0:T(8,128)(2,1)}), bf16[8,1024,512]{2,1,0:T(8,128)(2,1)}) %all-gather.8.cloned.1.call-update) | async-done | bytes 8388624 | tf_op jit(solution)/shard_map/all_gather | solution.py:611
  158.9 31.1 %memory_forward.1 = (bf16[2048,256]{1,0:T(8,128)(2,1)}, f32[2048,256]{1,0:T(8,128)}, f32[2048,256]{1,0:T(8,128)}) custom-call(s32[5]{0:T(128)} %pad_add_fusion.chosen, bf16[2048,256]{1,0:T(8,128)(2,1)} %get-tuple-element.61.q_ref, f32[2048,256]{1,0:T(8,128)} %get-tuple-element.20.mix_ref, f32[2048,256]{1,0:T(8,128)} %get-tuple-element.21.max_ref, ...), custom_call_target="tpu_custom_call" | custom-call | flops 17179869184 | bytes 18874368 | tf_op jit(solution)/shard_map/memory_forward/pallas_call | solution.py:427
  192.4 14.2 %all_to_all.77 = bf16[4,512,256]{1,2,0:T(8,128)(2,1)S(1)} all-to-all(bf16[4,512,256]{1,2,0:T(8,128)(2,1)} %copy.54), channel_id=1, replica_groups=mesh['seg'=8,'seq'=4] {'seq'}, dimensions={0} | all-to-all | bytes 2097152 | tf_op jit(solution)/shard_map/all_to_all | solution.py:635
  218.3 11.7 %multiply_convert_fusion = (bf16[512,2816]{1,0:T(8,128)(2,1)}, bf16[512,2816]{1,0:T(8,128)(2,1)}, bf16[512,2816]{1,0:T(8,128)(2,1)}) fusion(f32[512,2816]{1,0:T(8,128)} %fusion.33, f32[512,2816]{1,0:T(8,128)} %fusion.34, bf16[2816,1024]{1,0:T(8,128)(2,1)} %param.21, bf16[1,512,1024]{2,1,0:T(8,128)(2,1)S(1)} %copy-done.20), kind=kOutput, calls=%fused_computation.6 | convolution fusion | flops 2974416896 | bytes 27000832 | tf_op jit(solution)/shard_map/dot_general | solution.py:26
  230.1 5.1 fusion.35
  240.9 5.6 all_to_all.78
  248.0 5.3 convolution_convert_fusion.2
  253.7 8.4 %all_to_all.79 = bf16[2,4,128,2816]{3,2,1,0:T(8,128)(2,1)S(1)} all-to-all(bf16[2,4,128,2816]{3,2,1,0:T(8,128)(2,1)S(1)} %bitcast.143), channel_id=1, replica_groups={{0,4},{8,12},{16,20},{24,28},{1,5},{9,13},{17,21},{25,29},{2,6},{10,14}..., dimensions={0} | all-to-all | bytes 11534336 | tf_op jit(solution)/shard_map/all_to_all | solution.py:571
  264.4 5.4 convolution_convert_fusion.1
  270.2 8.4 %all_to_all.80 = bf16[2,4,128,2816]{3,2,1,0:T(8,128)(2,1)S(1)} all-to-all(bf16[2,4,128,2816]{3,2,1,0:T(8,128)(2,1)S(1)} %bitcast.144), channel_id=1, replica_groups={{0,4},{8,12},{16,20},{24,28},{1,5},{9,13},{17,21},{25,29},{2,6},{10,14}..., dimensions={0} | all-to-all | bytes 11534336 | tf_op jit(solution)/shard_map/all_to_all | solution.py:571
  289.0 9.5 %all_to_all.81 = bf16[2,4,352,1024]{3,2,1,0:T(8,128)(2,1)} all-to-all(bf16[2,4,352,1024]{3,2,1,0:T(8,128)(2,1)S(1)} %bitcast.145), channel_id=1, replica_groups={{0,4},{8,12},{16,20},{24,28},{1,5},{9,13},{17,21},{25,29},{2,6},{10,14}..., dimensions={0} | all-to-all | bytes 11534336 | tf_op jit(solution)/shard_map/all_to_all | solution.py:571
  302.1 5.8 fusion.3
  308.3 8.2 %all-to-all-done.2 = bf16[512,4,256]{2,0,1:T(8,128)(2,1)S(1)} async-done(((bf16[512,4,256]{2,0,1:T(8,128)(2,1)}), bf16[512,4,256]{2,0,1:T(8,128)(2,1)S(1)}, u32[]{:S(2)}, u32[]{:S(2)}) %all-to-all-start.2) | async-done | bytes 1048608 | tf_op jit(solution)/shard_map/all_to_all | solution.py:661
  317.5 34.9 %memory_backward.1 = (f32[2048,256]{1,0:T(8,128)}, f32[2048,256]{1,0:T(8,128)}) custom-call(s32[5]{0:T(128)} %pad_add_fusion.chosen, bf16[2048,256]{1,0:T(8,128)(2,1)} %get-tuple-element.61.q_ref, bf16[2048,256]{1,0:T(8,128)(2,1)} %bitcast.169, f32[2048,256]{1,0:T(8,128)} %get-tuple-element.25.out_ref, f32[2048,256]{1,0:T(8,128)} %get-tuple-element.24.log_ref, ...), custom_call_target="tpu_custom_call" | custom-call | flops 25769803776 | bytes 18874368 | tf_op jit(solution)/shard_map/memory_backward/pallas_call | solution.py:478
  352.4 24.0 %own_backward.1 = (f32[2048,256]{1,0:T(8,128)}, f32[2048,256]{1,0:T(8,128)}, f32[2048,256]{1,0:T(8,128)}) custom-call(bf16[2048,256]{1,0:T(8,128)(2,1)} %get-tuple-element.61.q_ref, bf16[2048,256]{1,0:T(8,128)(2,1)} %get-tuple-element.60.k_ref, bf16[2048,256]{1,0:T(8,128)(2,1)} %slice.119.v_ref, bf16[2048,256]{1,0:T(8,128)(2,1)} %bitcast.170, ...), custom_call_target="tpu_custom_call" | custom-call | flops 10737418240 | bytes 18874368 | tf_op jit(solution)/shard_map/own_backward/pallas_call | solution.py:536
  389.9 5.8 maximum_multiply_fusion.2
  398.0 23.4 %reduce-scatter.22.cloned.1.call-done = bf16[1,352,1024]{2,1,0:T(8,128)(2,1)} async-done(((bf16[4,352,1024]{2,1,0:T(8,128)(2,1)}), bf16[1,352,1024]{2,1,0:T(8,128)(2,1)}) %reduce-scatter.22.cloned.1.call-update) | async-done | bytes 720912
  421.5 6.8 convolution_convert_fusion.5
  430.2 22.1 %all_to_all.82 = bf16[4,256,768]{1,2,0:T(8,128)(2,1)S(1)} all-to-all(bf16[4,256,768]{1,2,0:T(8,128)(2,1)S(1)} %copy.56), channel_id=1, replica_groups=mesh['seg'=8,'seq'=4] {'seq'}, dimensions={0} | all-to-all | bytes 3145728 | tf_op jit(solution)/shard_map/all_to_all | solution.py:680
  454.3 6.6 convolution_convert_fusion.3
  460.9 60.1 %all-reduce.10.cloned.1.call-done = (bf16[1,128,1024]{2,1,0:T(8,128)(2,1)}, bf16[1,128,2816]{2,1,0:T(8,128)(2,1)}, bf16[1,128,2816]{2,1,0:T(8,128)(2,1)}, bf16[1,352,1024]{2,1,0:T(8,128)(2,1)}) async-done(((bf16[1,128,1024]{2,1,0:T(8,128)(2,1)}, bf16[1,128,2816]{2,1,0:T(8,128)(2,1)}, bf16[1,128,2816]{2,1,0:T(8,128)(2,1)}, bf16[1,352,1024]{2,1,0:T(8,128)(2,1)}), (bf16[1,128,1024]{2,1,0:T(8,128)(2,1)}, ...) | async-done | bytes 2424848 | tf_op jit(solution)/shard_map/psum | solution.py:574
  521.9 7.6 %fusion.19 = bf16[1,512,1024]{2,1,0:T(8,128)(2,1)} fusion(f32[512,1024]{1,0:T(8,128)S(1)} %copy-done.5, bf16[512,2816]{1,0:T(8,128)(2,1)} %get-tuple-element.59, bf16[2816,1024]{1,0:T(8,128)(2,1)} %param.21), kind=kOutput, calls=%fused_computation.73 | convolution fusion | flops 2953838592 | bytes 11796480 | tf_op jit(solution)/shard_map/dot_general | solution.py:22
  529.5 55.2 %all-reduce.8.cloned.1.call-done = bf16[256,3072]{0,1:T(8,128)(2,1)} async-done(((bf16[256,3072]{0,1:T(8,128)(2,1)}), bf16[256,3072]{0,1:T(8,128)(2,1)}) %all-reduce.8.cloned.1.call-update) | async-done | bytes 1572880 | tf_op jit(solution)/shard_map/psum | solution.py:684
  591.3 48.3 %reduce-scatter.14.cloned.1.call-done = bf16[512,1024]{1,0:T(8,128)(2,1)} async-done(((bf16[2048,1024]{1,0:T(8,128)(2,1)}), bf16[512,1024]{1,0:T(8,128)(2,1)}) %reduce-scatter.14.cloned.1.call-update) | async-done | bytes 1048592 | tf_op jit(solution)/shard_map/reduce_scatter | solution.py:676
  641.8 39.4 %psum.42 = f32[2,1024]{1,0:T(2,128)S(1)} all-reduce(f32[2,1024]{1,0:T(2,128)S(1)} %pad_maximum_fusion.5), channel_id=1, replica_groups=mesh['seg'=8,'seq'=4] {'seg','seq'}, use_global_device_ids=true, to_apply=%region_7.8 | all-reduce | flops 2048 | bytes 16384 | tf_op jit(solution)/shard_map/psum | solution.py:688
  (181 shorter events, 117.3 us)
Async XLA Ops:
  7.2 199.5 %copy-start = (bf16[1024,1024]{1,0:T(8,128)(2,1)S(1)}, bf16[1024,1024]{1,0:T(8,128)(2,1)}, u32[]{:S(2)}) copy-start(bf16[1024,1024]{1,0:T(8,128)(2,1)} %param.18) | copy-start | bytes 6291460
  7.2 68.1 %all-gather.6.cloned.1.call-start = ((), (), s32[]{:S(2)}) async-start(), calls=%async_computation.13 | async-start | bytes 5242880 | tf_op jit(solution)/shard_map/all_gather | solution.py:616
  12.6 146.3 %all-gather.8.cloned.1.call-start = ((), (), s32[]{:S(2)}) async-start(), calls=%async_computation.14 | async-start | bytes 9437184 | tf_op jit(solution)/shard_map/all_gather | solution.py:611
  14.8 27.6 %copy-start.33 = (s32[8]{0:T(128)S(1)}, s32[8]{0:T(128)}, u32[]{:S(2)}) copy-start(s32[8]{0:T(128)} %param.24) | copy-start | bytes 100
  14.8 28.2 %copy-start.32 = (s32[8,3]{0,1:T(4,128)S(1)}, s32[8,3]{0,1:T(4,128)}, u32[]{:S(2)}) copy-start(s32[8,3]{0,1:T(4,128)} %param.25) | copy-start | bytes 292
  42.3 355.7 %reduce-scatter.16.cloned.1.call-start = ((), (), s32[]{:S(2)}) async-start(), calls=%async_computation.20 | async-start | bytes 1310720
  99.0 8.3 %slice-start = ((s8[6291456]{0:T(1024)(128)(4,1)}), s8[4194304]{0:T(1024)(128)(4,1)S(1)}, s32[]{:S(2)}) async-start(s8[6291456]{0:T(1024)(128)(4,1)} %bitcast.148), calls=%async_computation.25 | async-start | bytes 8388608
  99.1 6.3 copy-start.16
  99.1 8.2 %slice-start.1 = ((s8[6291456]{0:T(1024)(128)(4,1)}), s8[2097152]{0:T(1024)(128)(4,1)S(1)}, s32[]{:S(2)}) async-start(s8[6291456]{0:T(1024)(128)(4,1)} %bitcast.148), calls=%async_computation.26 | async-start | bytes 4194304
  190.0 16.6 %copy-start.2 = (bf16[1,512,1024]{2,1,0:T(8,128)(2,1)S(1)}, bf16[1,512,1024]{2,1,0:T(8,128)(2,1)}, u32[]{:S(2)}) copy-start(bf16[1,512,1024]{2,1,0:T(8,128)(2,1)} %param.13) | copy-start | bytes 3145732
  192.4 15.9 %slice-start.2 = ((s8[5767168]{0:T(1024)(128)(4,1)}), s8[4194304]{0:T(1024)(128)(4,1)S(1)}, s32[]{:S(2)}) async-start(s8[5767168]{0:T(1024)(128)(4,1)} %bitcast.177), calls=%async_computation.27 | async-start | bytes 8388608
  208.0 30.7 %copy-start.4 = (f32[512,1024]{1,0:T(8,128)}, f32[512,1024]{1,0:T(8,128)S(1)}, u32[]{:S(2)}) copy-start(f32[512,1024]{1,0:T(8,128)S(1)} %get-tuple-element.88) | copy-start | bytes 6291460
  247.9 150.1 %reduce-scatter.18.cloned.1.call-start = ((), (), s32[]{:S(2)}) async-start(), calls=%async_computation.21 | async-start | bytes 3604480
  264.4 133.7 %reduce-scatter.20.cloned.1.call-start = ((), (), s32[]{:S(2)}) async-start(), calls=%async_computation.22 | async-start | bytes 3604480
  298.5 18.0 %all-to-all-start.2 = ((bf16[512,4,256]{2,0,1:T(8,128)(2,1)}), bf16[512,4,256]{2,0,1:T(8,128)(2,1)S(1)}, u32[]{:S(2)}, u32[]{:S(2)}) async-start(bf16[512,4,256]{2,0,1:T(8,128)(2,1)} %bitcast.142), calls=%async_computation.2 | async-start | bytes 2097152 | tf_op jit(solution)/shard_map/all_to_all | solution.py:661
  302.1 119.3 %reduce-scatter.22.cloned.1.call-start = ((), (), s32[]{:S(2)}) async-start(), calls=%async_computation.23 | async-start | bytes 3604480
  307.9 213.2 %all-reduce.10.cloned.1.call-start = ((), (), s32[]{:S(2)}) async-start(), calls=%async_computation.24 | async-start | bytes 4849664 | tf_op jit(solution)/shard_map/psum | solution.py:574
  398.0 23.5 %copy-start.21 = (bf16[2048,256]{1,0:T(8,128)(2,1)S(1)}, bf16[2048,256]{1,0:T(8,128)(2,1)}, u32[]{:S(2)}) copy-start(bf16[2048,256]{1,0:T(8,128)(2,1)} %get-tuple-element.64) | copy-start | bytes 3145732
  398.0 23.5 %copy-start.22 = (bf16[2048,256]{1,0:T(8,128)(2,1)S(1)}, bf16[2048,256]{1,0:T(8,128)(2,1)}, u32[]{:S(2)}) copy-start(bf16[2048,256]{1,0:T(8,128)(2,1)} %get-tuple-element.65) | copy-start | bytes 3145732
  421.4 163.4 %all-reduce.8.cloned.1.call-start = ((), (), s32[]{:S(2)}) async-start(), calls=%async_computation.16 | async-start | bytes 3145728 | tf_op jit(solution)/shard_map/psum | solution.py:684
  453.6 186.0 %reduce-scatter.14.cloned.1.call-start = ((), (), s32[]{:S(2)}) async-start(), calls=%async_computation.15 | async-start | bytes 5242880 | tf_op jit(solution)/shard_map/reduce_scatter | solution.py:676
  460.9 61.0 %copy-start.5 = (f32[512,1024]{1,0:T(8,128)S(1)}, f32[512,1024]{1,0:T(8,128)}, u32[]{:S(2)}) copy-start(f32[512,1024]{1,0:T(8,128)} %copy-done.4) | copy-start | bytes 6291460
  460.9 224.4 %all-gather.10.cloned.1.call-start = ((), (), s32[]{:S(2)}) async-start(), calls=%async_computation.17 | async-start | bytes 2162688 | tf_op jit(solution)/shard_map/all_gather | solution.py:575
  521.1 167.4 %all-gather.12.cloned.1.call-start = ((), (), s32[]{:S(2)}) async-start(), calls=%async_computation.18 | async-start | bytes 2162688 | tf_op jit(solution)/shard_map/all_gather | solution.py:575
  521.8 169.9 %all-gather.14.cloned.1.call-start = ((), (), s32[]{:S(2)}) async-start(), calls=%async_computation.19 | async-start | bytes 2162688 | tf_op jit(solution)/shard_map/all_gather | solution.py:575
  529.5 58.3 %copy-start.26 = (bf16[1,128,1024]{2,1,0:T(8,128)(2,1)S(1)}, bf16[1,128,1024]{2,1,0:T(8,128)(2,1)}, u32[]{:S(2)}) copy-start(bf16[1,128,1024]{2,1,0:T(8,128)(2,1)} %get-tuple-element.53) | copy-start | bytes 786436
  587.8 51.7 %copy-start.3 = (bf16[1,512,1024]{2,1,0:T(8,128)(2,1)S(1)}, bf16[1,512,1024]{2,1,0:T(8,128)(2,1)}, u32[]{:S(2)}) copy-start(bf16[1,512,1024]{2,1,0:T(8,128)(2,1)} %param.13) | copy-start | bytes 3145732
  587.8 51.7 %copy-start.27 = (f32[1024]{0:T(1024)S(1)}, f32[1024]{0:T(1024)}, u32[]{:S(2)}) copy-start(f32[1024]{0:T(1024)} %param.15) | copy-start | bytes 12292
  587.8 51.7 %copy-start.29 = (f32[512]{0:T(512)S(1)}, f32[512]{0:T(512)}, u32[]{:S(2)}) copy-start(f32[512]{0:T(512)} %copy-done.28) | copy-start | bytes 6148
  590.1 91.7 %copy-start.31 = (f32[512]{0:T(512)S(1)}, f32[512]{0:T(512)}, u32[]{:S(2)}) copy-start(f32[512]{0:T(512)} %get-tuple-element.83) | copy-start | bytes 6148
  639.6 42.2 %copy-start.17 = (bf16[512,1024]{1,0:T(8,128)(2,1)S(1)}, bf16[512,1024]{1,0:T(8,128)(2,1)}, u32[]{:S(2)}) copy-start(bf16[512,1024]{1,0:T(8,128)(2,1)} %reduce-scatter.14.cloned.1.call-done) | copy-start | bytes 3145732
  688.4 6.6 copy-start.1
  (23 other events, 80.7 us)
Sparse Core Ops, SparseCore 0:
  12.8 62.4 all-gather.5
  76.9 82.0 all-gather.7
  248.0 29.7 reduce-scatter.15
  281.3 49.5 reduce-scatter.17
  334.4 41.7 reduce-scatter.19
  379.6 41.7 reduce-scatter.21
  424.0 97.0 all-reduce.9
  524.0 60.7 all-reduce.7
  587.7 51.7 reduce-scatter.13
  640.9 9.6 all-gather.9
  652.2 10.7 all-gather.11
  664.4 10.7 all-gather.13
